TPU v7x, 32 devices: a whole 2x2x4 slice. The times are simulated.
32 devices in a mesh: rep: 4 (over y, core), dp: 8 (over z, x).
Axes of the slice: x: 2, y: 2, z: 4, core: 2. Of those that a mesh axis runs over, the one named last changes fastest.
Arguments:
- query_states: bfloat16 [256, 32, 768], P(('rep', 'dp')), may hold values from -12 to 12
- passage_states: bfloat16 [128, 180, 768], P(('rep', 'dp')), may hold values from -12 to 12
- query_lengths: int32 [256], P(('rep', 'dp')), may hold values from 8 to 32, as said below
- passage_lengths: int32 [128], P(('rep', 'dp')), may hold values from 45 to 180, as said below
- passage_ids: int32 [128, 180], P(('rep', 'dp')), may hold values from 2 to 30521, as said below
- positives: int32 [256], P(('rep', 'dp')), may hold values from 0 to 31, as said below
- up_weight: bfloat16 [768, 3072], replicated, may hold values from -0.21875 to 0.21875
- up_bias: float32 [3072], replicated, may hold values from -3 to 3
- down_weight: bfloat16 [3072, 768], replicated, may hold values from -0.109375 to 0.109375
- down_bias: float32 [768], replicated, may hold values from -3 to 3
- norm_gain: float32 [768], replicated, may hold values from 0.5 to 1.5
- norm_bias: float32 [768], replicated, may hold values from -2 to 2
- proj_weight: bfloat16 [768, 128], replicated, may hold values from -0.21875 to 0.21875
Outputs:
- mean_loss: float32 [], replicated
- passage_grad: float32 [128, 180, 128], P(('rep', 'dp'))
- proj_grad: float32 [768, 128], replicated
Inputs may be any that keep to these rules, and one draw needn't show every extreme that they name: `query_lengths`: every device holds a query with all 32 slots real. `passage_lengths`: every device holds a passage with all 180 slots real. `passage_ids`: slots 0 and 1 of every passage hold ids 101 and 2; ids 999 to 1066 are punctuation. `positives`: index of the positive passage among the 32 passages of the query's replica group, in the order of the devices.
All inputs are finite; a program needn't handle non-finite values.
Results may differ from a plain program's by a relative error of at most 0.0055.
Values may be sent and summed in bfloat16 or wider, within the bound.
A program may use at most 128 MiB of HBM per device.

v0:
```python
import math
import jax
import jax.numpy as jnp
from jax import lax
from jax.sharding import PartitionSpec as P

temper = 0.05
eps_norm = 1e-06
punct_low = 999
punct_high = 1067


def encode_rows(
    token_rows, up_weight, up_bias, down_weight, down_bias, norm_gain, norm_bias, proj_weight
):
    upward = jnp.dot(token_rows, up_weight, preferred_element_type=jnp.float32) + up_bias
    activated = jax.nn.gelu(upward, approximate=False).astype(jnp.bfloat16)
    residual = (
        token_rows.astype(jnp.float32)
        + jnp.dot(activated, down_weight, preferred_element_type=jnp.float32)
        + down_bias
    )
    average = jnp.mean(residual, -1, keepdims=True)
    centered = residual - average
    variance = jnp.mean(centered * centered, -1, keepdims=True)
    hidden = (centered * lax.rsqrt(variance + eps_norm) * norm_gain + norm_bias).astype(
        jnp.bfloat16
    )
    projected = jnp.dot(hidden, proj_weight, preferred_element_type=jnp.float32)
    inverse = lax.rsqrt(jnp.sum(projected * projected, -1, keepdims=True) + eps_norm)
    return (hidden, projected * inverse, inverse)


def token_scores(query_flat, query_keep, block_emb, block_keep, query_count):
    item_count, pass_len, embed_dim = block_emb.shape
    flat_block = block_emb.reshape(item_count * pass_len, embed_dim)
    similar = lax.dot_general(
        query_flat, flat_block, (((1,), (1,)), ((), ())), preferred_element_type=jnp.float32
    )
    weights = (
        jnp.exp(similar / temper).reshape(-1, item_count, pass_len)
        * block_keep.astype(jnp.float32)[None]
    )
    totals = jnp.sum(weights, -1)
    soft_max = temper * jnp.log(totals) * query_keep[:, None]
    scores = jnp.sum(soft_max.reshape(query_count, -1, item_count), 1)
    return (scores, weights, totals)


def token_grads(query_flat, query_keep, block_emb, weights, totals, dscore, query_count):
    item_count, pass_len, embed_dim = block_emb.shape
    factor = (dscore[:, None, :] * query_keep.reshape(query_count, -1)[:, :, None]).reshape(
        -1, item_count
    ) / totals
    sim_grad = (
        (weights * factor[:, :, None]).reshape(-1, item_count * pass_len).astype(jnp.bfloat16)
    )
    flat_block = block_emb.reshape(item_count * pass_len, embed_dim)
    passage_term = lax.dot_general(
        sim_grad, query_flat, (((0,), (0,)), ((), ())), preferred_element_type=jnp.float32
    )
    query_term = jnp.dot(sim_grad, flat_block, preferred_element_type=jnp.float32)
    return (passage_term.reshape(item_count, pass_len, embed_dim), query_term)


def cross_entropy(scores, positives):
    log_total = jnp.log(jnp.sum(jnp.exp(scores), 1))
    onehot = (jnp.arange(scores.shape[1], dtype=jnp.int32)[None, :] == positives[:, None]).astype(
        jnp.float32
    )
    loss_sum = jnp.sum(log_total - jnp.sum(scores * onehot, 1))
    dscore = jnp.exp(scores - log_total[:, None]) - onehot
    return (loss_sum, dscore)


def norm_backward(gradient, normed, inverse):
    return (inverse * (gradient - normed * jnp.sum(normed * gradient, -1, keepdims=True))).astype(
        jnp.bfloat16
    )


def per_device(
    query_states,
    passage_states,
    query_lengths,
    passage_lengths,
    passage_ids,
    positives,
    up_weight,
    up_bias,
    down_weight,
    down_bias,
    norm_gain,
    norm_bias,
    proj_weight,
):
    query_count, query_len, model_width = query_states.shape
    pass_count, pass_len, _ = passage_states.shape
    embed_dim = proj_weight.shape[1]
    token_rows = jnp.concatenate(
        [query_states.reshape(-1, model_width), passage_states.reshape(-1, model_width)], 0
    )
    hidden, normed, inverse = encode_rows(
        token_rows, up_weight, up_bias, down_weight, down_bias, norm_gain, norm_bias, proj_weight
    )
    boundary = query_count * query_len
    query_emb = normed[:boundary].astype(jnp.bfloat16)
    pass_emb = normed[boundary:].astype(jnp.bfloat16).reshape(pass_count, pass_len, embed_dim)
    query_keep = (
        (jnp.arange(query_len, dtype=jnp.int32)[None, :] < query_lengths[:, None])
        .astype(jnp.float32)
        .reshape(-1)
    )
    is_punct = (passage_ids >= punct_low) & (passage_ids < punct_high)
    pass_keep = (
        (jnp.arange(pass_len, dtype=jnp.int32)[None, :] < passage_lengths[:, None])
        & jnp.logical_not(is_punct)
    ).astype(jnp.bfloat16)
    groups = lax.axis_size("dp")
    gathered, gathered_keep = (
        lax.all_gather(pass_emb, "dp", axis=0, tiled=True),
        lax.all_gather(pass_keep, "dp", axis=0, tiled=True),
    )
    group_pass = pass_count * groups
    block_pass = math.gcd(group_pass, 16)
    block_count = group_pass // block_pass
    emb_blocks = gathered.reshape(block_count, block_pass, pass_len, embed_dim)
    keep_blocks = gathered_keep.reshape(block_count, block_pass, pass_len)

    def forward(paired):
        scores, _, _ = token_scores(query_emb, query_keep, paired[0], paired[1], query_count)
        return scores

    stacked = lax.map(forward, (emb_blocks, keep_blocks))
    scores = jnp.transpose(stacked, (1, 0, 2)).reshape(query_count, group_pass)
    loss_sum, dscore = cross_entropy(scores, positives)
    grad_blocks = jnp.transpose(dscore.reshape(query_count, block_count, block_pass), (1, 0, 2))

    def backward(query_grad, triple):
        block_emb, block_keep, block_grad = triple
        _, weights, totals = token_scores(query_emb, query_keep, block_emb, block_keep, query_count)
        passage_term, query_term = token_grads(
            query_emb, query_keep, block_emb, weights, totals, block_grad, query_count
        )
        return (query_grad + query_term, passage_term)

    start_grad = jnp.zeros((query_count * query_len, embed_dim), jnp.float32)
    query_grad, pass_terms = lax.scan(backward, start_grad, (emb_blocks, keep_blocks, grad_blocks))
    passage_grad = lax.psum_scatter(
        pass_terms.reshape(group_pass, pass_len, embed_dim), "dp", scatter_dimension=0, tiled=True
    )
    query_back = norm_backward(query_grad, normed[:boundary], inverse[:boundary])
    pass_back = norm_backward(
        passage_grad.reshape(-1, embed_dim), normed[boundary:], inverse[boundary:]
    )
    all_back = jnp.concatenate([query_back, pass_back], 0)
    local_sum = lax.dot_general(
        hidden, all_back, (((0,), (0,)), ((), ())), preferred_element_type=jnp.float32
    )
    proj_total, loss_total = lax.psum((local_sum, loss_sum), ("rep", "dp"))
    mean_loss = loss_total / (query_count * lax.axis_size("rep") * groups)
    return (mean_loss, passage_grad, proj_total)


def solution(mesh):
    in_specs = (
        P(("rep", "dp"), None, None),
        P(("rep", "dp"), None, None),
        P(("rep", "dp")),
        P(("rep", "dp")),
        P(("rep", "dp"), None),
        P(("rep", "dp")),
        P(),
        P(),
        P(),
        P(),
        P(),
        P(),
        P(),
    )
    out_specs = (P(), P(("rep", "dp"), None, None), P())
    return jax.shard_map(
        per_device, mesh=mesh, in_specs=in_specs, out_specs=out_specs, check_vma=False
    )
```

profile of v0, /device:TPU:0, one launch (start us, length us, event | category | flops | bytes accessed | tf_op | source)
XLA Modules:
  0.0 375.2 jit_solution(12768285296816217812)
XLA Ops:
  9.8 39.0 %fusion.77 = (f32[976]{0:T(1024)S(1)}, f32[976,768]{1,0:T(8,128)S(1)}) fusion(f32[768]{0:T(1024)} %param.26, bf16[3072,768]{1,0:T(8,128)(2,1)} %param.25, f32[3072]{0:T(1024)} %param.24, bf16[768,3072]{1,0:T(8,128)(2,1)} %param.23, bf16[720,768]{1,0:T(8,128)(2,1)} %reshape.166, bf16[256,768]{1,0:T(8,128)(2,1)} %bitcast.86), kind=kOutput, calls=%fused_computation.113 | convolution fusion | flops 9416821760 | bytes 13953856 | tf_op jit(solution)/shard_map/dot_general | solution.py:20
  53.0 27.9 %all-gather = bf16[8,4,180]{2,1,0:T(4,128)(2,1)S(1)} all-gather(bf16[1,4,180]{2,1,0:T(4,128)(2,1)S(1)} %fusion.42), channel_id=1, replica_groups=mesh['rep'=4,'dp'=8] {'dp'}, dimensions={0}, use_global_device_ids=true | all-gather | bytes 12960 | tf_op jit(solution)/shard_map/all_gather | solution.py:122
  80.9 18.3 %all-gather.3.cloned.1.call-done = bf16[32,180,128]{2,1,0:T(8,128)(2,1)} async-done(((bf16[4,180,128]{2,1,0:T(8,128)(2,1)}), bf16[32,180,128]{2,1,0:T(8,128)(2,1)}) %all-gather.3.cloned.1.call-update) | async-done | bytes 1474576 | tf_op jit(solution)/shard_map/all_gather | solution.py:121
  99.3 13.9 %while.24 = (s32[]{:T(128)}, f32[2,8,16]{2,1,0:T(8,128)S(1)}, bf16[2,16,180,128]{3,2,1,0:T(8,128)(2,1)}, bf16[256,128]{1,0:T(8,128)(2,1)S(1)}, bf16[2,16,180]{2,1,0:T(8,128)(2,1)S(1)}, /*index=5*/s32[8]{0:T(128)S(1)}, s32[]{:T(128)}) while((s32[]{:T(128)}, f32[2,8,16]{2,1,0:T(8,128)S(1)}, bf16[2,16,180,128]{3,2,1,0:T(8,128)(2,1)}, ...), condition=%wide.region_6.7_spmd.clone, body=%wide.region_3.6_spmd.clone.sunk | while | flops 190962880 | bytes 15687425 | solution.py:134
  100.7 2.2 fusion.106
  102.9 2.6 reshape.189
  107.6 2.2 fusion.106
  109.8 2.6 reshape.189
  114.1 45.3 %while.25 = (s32[]{:T(128)}, f32[256,128]{1,0:T(8,128)S(1)}, f32[2,16,180,128]{3,2,1,0:T(8,128)}, bf16[2,16,180,128]{3,2,1,0:T(8,128)(2,1)}, bf16[256,128]{1,0:T...) while((s32[]{:T(128)}, f32[256,128]{1,0:T(8,128)S(1)}, ...), condition=%wide.region_13.14_spmd.clone, body=%wide.region_11.13_spmd.clone.sunk | while | flops 570727744 | bytes 49299292 | solution.py:148
  118.5 1.8 reshape.191
  120.3 2.3 multiply_reduce_fusion.12
  122.7 1.9 mul.316
  124.5 4.1 %mul.317 = f32[256,2880]{0,1:T(8,128)} reshape(f32[256,16,180]{0,2,1:T(8,128)} %mul.316) | data formatting | bytes 5898240 | tf_op jit(solution)/shard_map/while/body/eval_jaxpr/mul | solution.py:56
  128.7 2.3 multiply_convert_fusion.4
  132.8 2.3 reshape.192
  141.2 1.8 reshape.191
  143.0 2.3 multiply_reduce_fusion.12
  145.3 1.9 mul.316
  147.2 4.1 %mul.317 = f32[256,2880]{0,1:T(8,128)} reshape(f32[256,16,180]{0,2,1:T(8,128)} %mul.316) | data formatting | bytes 5898240 | tf_op jit(solution)/shard_map/while/body/eval_jaxpr/mul | solution.py:56
  151.3 2.3 multiply_convert_fusion.4
  155.5 2.3 reshape.192
  161.7 70.0 %reduce-scatter.2.cloned.1.call-done = f32[4,180,128]{2,1,0:T(8,128)} async-done(((f32[32,180,128]{2,1,0:T(8,128)}), f32[4,180,128]{2,1,0:T(8,128)}) %reduce-scatter.2.cloned.1.call-update) | async-done | bytes 368656 | tf_op jit(solution)/shard_map/reduce_scatter | solution.py:149
  235.6 39.9 %psum.14 = f32[]{:T(128)} all-reduce(f32[]{:T(128)} %get-tuple-element.165), channel_id=1, replica_groups=mesh['rep'=4,'dp'=8] {'rep','dp'}, use_global_device_ids=true, to_apply=%region_10.11 | all-reduce | flops 1 | bytes 8 | tf_op jit(solution)/shard_map/psum | solution.py:160
  277.0 88.8 %all-reduce.2.cloned.1.call-done = f32[768,128]{1,0:T(8,128)} async-done(((f32[768,128]{1,0:T(8,128)}), f32[768,128]{1,0:T(8,128)}) %all-reduce.2.cloned.1.call-update) | async-done | bytes 393232 | tf_op jit(solution)/shard_map/psum | solution.py:160
  (117 shorter events, 36.1 us)
Async XLA Ops:
  7.2 43.8 %copy-start = (bf16[768,128]{1,0:T(8,128)(2,1)S(1)}, bf16[768,128]{1,0:T(8,128)(2,1)}, u32[]{:S(2)}) copy-start(bf16[768,128]{1,0:T(8,128)(2,1)} %param.29) | copy-start | bytes 589828
  7.2 92.1 %all-gather.3.cloned.1.call-start = ((), (), s32[]{:S(2)}) async-start(), calls=%async_computation.1 | async-start | bytes 1695744 | tf_op jit(solution)/shard_map/all_gather | solution.py:121
  9.7 39.6 %copy-start.10 = (f32[768]{0:T(1024)S(1)}, f32[768]{0:T(1024)}, u32[]{:S(2)}) copy-start(f32[768]{0:T(1024)} %param.28) | copy-start | bytes 9220
  9.8 39.6 %copy-start.11 = (f32[768]{0:T(1024)S(1)}, f32[768]{0:T(1024)}, u32[]{:S(2)}) copy-start(f32[768]{0:T(1024)} %param.27) | copy-start | bytes 9220
  49.3 3.6 copy-start.9
  49.3 3.6 copy-start.13
  49.3 50.0 %copy-start.8 = (s32[8]{0:T(128)S(1)}, s32[8]{0:T(128)}, u32[]{:S(2)}) copy-start(s32[8]{0:T(128)} %param.19) | copy-start | bytes 100
  49.9 1.1 copy-start.3
  51.9 47.4 %copy-start.5 = (f32[976,128]{1,0:T(8,128)}, f32[976,128]{1,0:T(8,128)S(1)}, u32[]{:S(2)}) copy-start(f32[976,128]{1,0:T(8,128)S(1)} %broadcast_multiply_fusion) | copy-start | bytes 1499140
  52.8 178.9 %reduce-scatter.2.cloned.1.call-start = ((), (), s32[]{:S(2)}) async-start(), calls=%async_computation.2 | async-start | bytes 3391488 | tf_op jit(solution)/shard_map/reduce_scatter | solution.py:149
  99.3 13.9 %copy-start.12 = (s32[8]{0:T(128)S(1)}, s32[8]{0:T(128)}, u32[]{:S(2)}) copy-start(s32[8]{0:T(128)} %param.22) | copy-start | bytes 100
  128.7 3.5 copy-start.2
  131.0 1.1 copy-start.1
  151.3 3.5 copy-start.2
  153.7 1.1 copy-start.1
  159.4 74.5 %copy-start.6 = (f32[976,128]{1,0:T(8,128)S(1)}, f32[976,128]{1,0:T(8,128)}, u32[]{:S(2)}) copy-start(f32[976,128]{1,0:T(8,128)} %copy-done.5) | copy-start | bytes 1499140
  159.4 74.8 %copy-start.4 = (bf16[976,768]{1,0:T(8,128)(2,1)S(1)}, bf16[976,768]{1,0:T(8,128)(2,1)}, u32[]{:S(2)}) copy-start(bf16[976,768]{1,0:T(8,128)(2,1)} %copy-done.3) | copy-start | bytes 4497412
  159.4 206.4 %all-reduce.2.cloned.1.call-start = ((), (), s32[]{:S(2)}) async-start(), calls=%async_computation.3 | async-start | bytes 786432 | tf_op jit(solution)/shard_map/psum | solution.py:160
  231.7 44.5 %copy-start.7 = (f32[4,180,128]{2,1,0:T(8,128)S(1)}, f32[4,180,128]{2,1,0:T(8,128)}, u32[]{:S(2)}) copy-start(f32[4,180,128]{2,1,0:T(8,128)} %reduce-scatter.2.cloned.1.call-done) | copy-start | bytes 1105924
Sparse Core Ops, SparseCore 0:
  52.9 46.3 all-gather.2
  159.6 72.0 reduce-scatter.1
  237.6 128.1 all-reduce.1
where the time goes:
time: 376 us; the launch traced here: 375 us
  waiting for transfers between devices  177 us (47%)
  blocking collectives  67.8 us (18%)
  matrix products  53.4 us (14%)
  local copies, waits for them, and re-layouts  44.1 us (12%)
  other arithmetic  16.6 us (4%)
  between operations  15.8 us (4%)
    psum x1, waiting for transfers between devices, per_device(): proj_total, loss_total = lax.psum((local_sum, loss_sum), ('rep', 'dp'))  88.8 us
    reduce_scatter x1, waiting for transfers between devices, per_device(): lax.psum_scatter(pass_terms.reshape(group_pass, pass_len, embed_dim), 'dp...  70 us
    psum x1, blocking collectives, per_device(): proj_total, loss_total = lax.psum((local_sum, loss_sum), ('rep', 'dp'))  39.9 us
    dot_general x1, matrix products, encode_rows(): jnp.dot(activated, down_weight, preferred_element_type=jnp.float32)  39 us
    all_gather x1, blocking collectives, per_device(): lax.all_gather(pass_keep, 'dp', axis=0, tiled=True)  27.9 us
    all_gather x1, waiting for transfers between devices, per_device(): lax.all_gather(pass_emb, 'dp', axis=0, tiled=True)  18.3 us
    mul x4, local copies, waits for them, and re-layouts, token_grads(): weights * factor[:, :, None]  12 us
    reshape x4, local copies, waits for them, and re-layouts, token_scores(): jnp.exp(similar / temper).reshape(-1, item_count, pass_len)  8.91 us
  transfers between devices with their start and end apart: 3, of which 3 were waited for; matrix products, arithmetic and copies ran while one was open for 1% of the time, Pallas kernels for 0%

commit v1 on v0

--- a/solution.py
+++ b/solution.py
@@ -157,7 +157,7 @@
     local_sum = lax.dot_general(
         hidden, all_back, (((0,), (0,)), ((), ())), preferred_element_type=jnp.float32
     )
-    proj_total, loss_total = lax.psum((local_sum, loss_sum), ("rep", "dp"))
+    proj_total, loss_total = lax.psum(lax.psum((local_sum, loss_sum), "dp"), "rep")
     mean_loss = loss_total / (query_count * lax.axis_size("rep") * groups)
     return (mean_loss, passage_grad, proj_total)
 

time: 376 us -> 351 us (0.934)
  blocking collectives: 67.8 us -> 54.3 us
  waiting for transfers between devices: 177 us -> 166 us
    psum x1 -> x2, blocking collectives: 39.9 us -> 26.3 us  [the longest x1 20.1 us: per_device(): lax.psum((local_sum, loss_sum), 'dp')]
    psum x1 -> x2, waiting for transfers between devices: 88.8 us -> 77.4 us  [the longest x1 71.2 us: per_device(): lax.psum((local_sum, loss_sum), 'dp')]
  transfers between devices with their start and end apart: 3 -> 4, of which waited for: 3 -> 4; matrix products, arithmetic and copies ran while one was open for 1% -> 1% of each run, Pallas kernels for 0% -> 0%
where the time goes in v1:
time: 351 us; the launch traced here: 350 us
  waiting for transfers between devices  166 us (47%)
  blocking collectives  54.3 us (15%)
  matrix products  53.4 us (15%)
  local copies, waits for them, and re-layouts  44.1 us (13%)
  other arithmetic  16.6 us (5%)
  between operations  15.8 us (5%)
    psum x1, waiting for transfers between devices, per_device(): lax.psum((local_sum, loss_sum), 'dp')  71.2 us
    reduce_scatter x1, waiting for transfers between devices, per_device(): lax.psum_scatter(pass_terms.reshape(group_pass, pass_len, embed_dim), 'dp...  70 us
    dot_general x1, matrix products, encode_rows(): jnp.dot(activated, down_weight, preferred_element_type=jnp.float32)  39 us
    all_gather x1, blocking collectives, per_device(): lax.all_gather(pass_keep, 'dp', axis=0, tiled=True)  27.9 us
    psum x1, blocking collectives, per_device(): lax.psum((local_sum, loss_sum), 'dp')  20.1 us
    all_gather x1, waiting for transfers between devices, per_device(): lax.all_gather(pass_emb, 'dp', axis=0, tiled=True)  18.3 us
    mul x4, local copies, waits for them, and re-layouts, token_grads(): weights * factor[:, :, None]  12 us
    reshape x4, local copies, waits for them, and re-layouts, token_scores(): jnp.exp(similar / temper).reshape(-1, item_count, pass_len)  8.91 us
  transfers between devices with their start and end apart: 4, of which 4 were waited for; matrix products, arithmetic and copies ran while one was open for 1% of the time, Pallas kernels for 0%

profile of v1, /device:TPU:0, one launch (start us, length us, event | category | flops | bytes accessed | tf_op | source)
XLA Modules:
  0.0 350.3 jit_solution(7419014983253992372)
XLA Ops:
  9.8 39.0 %fusion.77 = (f32[976]{0:T(1024)S(1)}, f32[976,768]{1,0:T(8,128)S(1)}) fusion(f32[768]{0:T(1024)} %param.26, bf16[3072,768]{1,0:T(8,128)(2,1)} %param.25, f32[3072]{0:T(1024)} %param.24, bf16[768,3072]{1,0:T(8,128)(2,1)} %param.23, bf16[720,768]{1,0:T(8,128)(2,1)} %reshape.166, bf16[256,768]{1,0:T(8,128)(2,1)} %bitcast.86), kind=kOutput, calls=%fused_computation.113 | convolution fusion | flops 9416821760 | bytes 13953856 | tf_op jit(solution)/shard_map/dot_general | solution.py:20
  53.0 27.9 %all-gather = bf16[8,4,180]{2,1,0:T(4,128)(2,1)S(1)} all-gather(bf16[1,4,180]{2,1,0:T(4,128)(2,1)S(1)} %fusion.42), channel_id=1, replica_groups=mesh['rep'=4,'dp'=8] {'dp'}, dimensions={0}, use_global_device_ids=true | all-gather | bytes 12960 | tf_op jit(solution)/shard_map/all_gather | solution.py:122
  80.9 18.3 %all-gather.3.cloned.1.call-done = bf16[32,180,128]{2,1,0:T(8,128)(2,1)} async-done(((bf16[4,180,128]{2,1,0:T(8,128)(2,1)}), bf16[32,180,128]{2,1,0:T(8,128)(2,1)}) %all-gather.3.cloned.1.call-update) | async-done | bytes 1474576 | tf_op jit(solution)/shard_map/all_gather | solution.py:121
  99.3 13.9 %while.24 = (s32[]{:T(128)}, f32[2,8,16]{2,1,0:T(8,128)S(1)}, bf16[2,16,180,128]{3,2,1,0:T(8,128)(2,1)}, bf16[256,128]{1,0:T(8,128)(2,1)S(1)}, bf16[2,16,180]{2,1,0:T(8,128)(2,1)S(1)}, /*index=5*/s32[8]{0:T(128)S(1)}, s32[]{:T(128)}) while((s32[]{:T(128)}, f32[2,8,16]{2,1,0:T(8,128)S(1)}, bf16[2,16,180,128]{3,2,1,0:T(8,128)(2,1)}, ...), condition=%wide.region_6.7_spmd.clone, body=%wide.region_3.6_spmd.clone.sunk | while | flops 190962880 | bytes 15687425 | solution.py:134
  100.7 2.2 fusion.106
  102.9 2.6 reshape.189
  107.6 2.2 fusion.106
  109.8 2.6 reshape.189
  114.1 45.3 %while.25 = (s32[]{:T(128)}, f32[256,128]{1,0:T(8,128)S(1)}, f32[2,16,180,128]{3,2,1,0:T(8,128)}, bf16[2,16,180,128]{3,2,1,0:T(8,128)(2,1)}, bf16[256,128]{1,0:T...) while((s32[]{:T(128)}, f32[256,128]{1,0:T(8,128)S(1)}, ...), condition=%wide.region_14.15_spmd.clone, body=%wide.region_12.14_spmd.clone.sunk | while | flops 570727744 | bytes 49299292 | solution.py:148
  120.3 2.3 multiply_reduce_fusion.12
  122.7 1.9 mul.316
  124.5 4.1 %mul.317 = f32[256,2880]{0,1:T(8,128)} reshape(f32[256,16,180]{0,2,1:T(8,128)} %mul.316) | data formatting | bytes 5898240 | tf_op jit(solution)/shard_map/while/body/eval_jaxpr/mul | solution.py:56
  128.7 2.3 multiply_convert_fusion.4
  132.8 2.3 reshape.192
  143.0 2.3 multiply_reduce_fusion.12
  145.3 1.9 mul.316
  147.2 4.1 %mul.317 = f32[256,2880]{0,1:T(8,128)} reshape(f32[256,16,180]{0,2,1:T(8,128)} %mul.316) | data formatting | bytes 5898240 | tf_op jit(solution)/shard_map/while/body/eval_jaxpr/mul | solution.py:56
  151.3 2.3 multiply_convert_fusion.4
  155.5 2.3 reshape.192
  161.7 70.0 %reduce-scatter.2.cloned.1.call-done = f32[4,180,128]{2,1,0:T(8,128)} async-done(((f32[32,180,128]{2,1,0:T(8,128)}), f32[4,180,128]{2,1,0:T(8,128)}) %reduce-scatter.2.cloned.1.call-update) | async-done | bytes 368656 | tf_op jit(solution)/shard_map/reduce_scatter | solution.py:149
  235.7 71.2 %all-reduce.3.cloned.1.call-done = f32[768,128]{1,0:T(8,128)} async-done(((f32[768,128]{1,0:T(8,128)}), f32[768,128]{1,0:T(8,128)}) %all-reduce.3.cloned.1.call-update) | async-done | bytes 393232 | tf_op jit(solution)/shard_map/psum | solution.py:160
  306.8 20.1 %psum.28 = f32[]{:T(128)} all-reduce(f32[]{:T(128)} %get-tuple-element.165), channel_id=1, replica_groups=mesh['rep'=4,'dp'=8] {'dp'}, use_global_device_ids=true, to_apply=%region_10.11 | all-reduce | flops 1 | bytes 8 | tf_op jit(solution)/shard_map/psum | solution.py:160
  326.9 6.3 %psum.29 = f32[]{:T(128)} all-reduce(f32[]{:T(128)} %psum.28), channel_id=1, replica_groups=mesh['rep'=4,'dp'=8] {'rep'}, use_global_device_ids=true, to_apply=%region_11.12 | all-reduce | flops 1 | bytes 8 | tf_op jit(solution)/shard_map/psum | solution.py:160
  334.7 6.3 %all-reduce.5.cloned.1.call-done = f32[768,128]{1,0:T(8,128)} async-done(((f32[768,128]{1,0:T(8,128)}), f32[768,128]{1,0:T(8,128)}) %all-reduce.5.cloned.1.call-update) | async-done | bytes 393232 | tf_op jit(solution)/shard_map/psum | solution.py:160
  (121 shorter events, 39.8 us)
Async XLA Ops:
  7.2 43.8 %copy-start = (bf16[768,128]{1,0:T(8,128)(2,1)S(1)}, bf16[768,128]{1,0:T(8,128)(2,1)}, u32[]{:S(2)}) copy-start(bf16[768,128]{1,0:T(8,128)(2,1)} %param.29) | copy-start | bytes 589828
  7.2 92.1 %all-gather.3.cloned.1.call-start = ((), (), s32[]{:S(2)}) async-start(), calls=%async_computation.1 | async-start | bytes 1695744 | tf_op jit(solution)/shard_map/all_gather | solution.py:121
  9.7 39.6 %copy-start.10 = (f32[768]{0:T(1024)S(1)}, f32[768]{0:T(1024)}, u32[]{:S(2)}) copy-start(f32[768]{0:T(1024)} %param.28) | copy-start | bytes 9220
  9.8 39.6 %copy-start.11 = (f32[768]{0:T(1024)S(1)}, f32[768]{0:T(1024)}, u32[]{:S(2)}) copy-start(f32[768]{0:T(1024)} %param.27) | copy-start | bytes 9220
  49.3 3.6 %copy-start.9 = (s32[4,180]{1,0:T(4,128)S(1)}, s32[4,180]{1,0:T(4,128)}, u32[]{:S(2)}) copy-start(s32[4,180]{1,0:T(4,128)} %param.21) | copy-start | bytes 8644
  49.3 3.6 %copy-start.13 = (s32[4]{0:T(128)S(1)}, s32[4]{0:T(128)}, u32[]{:S(2)}) copy-start(s32[4]{0:T(128)} %param.20) | copy-start | bytes 52
  49.3 50.0 %copy-start.8 = (s32[8]{0:T(128)S(1)}, s32[8]{0:T(128)}, u32[]{:S(2)}) copy-start(s32[8]{0:T(128)} %param.19) | copy-start | bytes 100
  49.9 1.1 copy-start.3
  51.9 47.4 %copy-start.5 = (f32[976,128]{1,0:T(8,128)}, f32[976,128]{1,0:T(8,128)S(1)}, u32[]{:S(2)}) copy-start(f32[976,128]{1,0:T(8,128)S(1)} %broadcast_multiply_fusion) | copy-start | bytes 1499140
  52.8 178.9 %reduce-scatter.2.cloned.1.call-start = ((), (), s32[]{:S(2)}) async-start(), calls=%async_computation.2 | async-start | bytes 3391488 | tf_op jit(solution)/shard_map/reduce_scatter | solution.py:149
  99.3 13.9 %copy-start.12 = (s32[8]{0:T(128)S(1)}, s32[8]{0:T(128)}, u32[]{:S(2)}) copy-start(s32[8]{0:T(128)} %param.22) | copy-start | bytes 100
  128.7 3.5 copy-start.2
  131.0 1.1 copy-start.1
  151.3 3.5 copy-start.2
  153.7 1.1 copy-start.1
  159.4 74.5 %copy-start.6 = (f32[976,128]{1,0:T(8,128)S(1)}, f32[976,128]{1,0:T(8,128)}, u32[]{:S(2)}) copy-start(f32[976,128]{1,0:T(8,128)} %copy-done.5) | copy-start | bytes 1499140
  159.4 74.8 %copy-start.4 = (bf16[976,768]{1,0:T(8,128)(2,1)S(1)}, bf16[976,768]{1,0:T(8,128)(2,1)}, u32[]{:S(2)}) copy-start(bf16[976,768]{1,0:T(8,128)(2,1)} %copy-done.3) | copy-start | bytes 4497412
  159.4 147.4 %all-reduce.3.cloned.1.call-start = ((), (), s32[]{:S(2)}) async-start(), calls=%async_computation.3 | async-start | bytes 786432 | tf_op jit(solution)/shard_map/psum | solution.py:160
  231.7 102.1 %copy-start.7 = (f32[4,180,128]{2,1,0:T(8,128)S(1)}, f32[4,180,128]{2,1,0:T(8,128)}, u32[]{:S(2)}) copy-start(f32[4,180,128]{2,1,0:T(8,128)} %reduce-scatter.2.cloned.1.call-done) | copy-start | bytes 1105924
  235.6 105.3 %all-reduce.5.cloned.1.call-start = ((), (), s32[]{:S(2)}) async-start(), calls=%async_computation.4 | async-start | bytes 786432 | tf_op jit(solution)/shard_map/psum | solution.py:160
Sparse Core Ops, SparseCore 0:
  52.9 46.3 all-gather.2
  159.6 72.0 reduce-scatter.1
  235.7 71.0 all-reduce.2
  309.0 31.8 all-reduce.4
